TPU v7x, 32 devices: a whole 2x2x4 slice. The times are simulated.
32 devices in a mesh: grp: 2 (over y), chan: 4 (over z), sub: 4 (over x, core).
Axes of the slice: x: 2, y: 2, z: 4, core: 2. Of those that a mesh axis runs over, the one named last changes fastest.
Arguments:
- voltages: bfloat16 [2048, 2, 5504], P(('grp', 'chan', 'sub')), parts along dimension 0, may hold values from -6 to 6
- taps: float32 [1536], replicated, may hold values from -0.15625 to 0.15625
- input_id: int32 [1024], replicated, may hold values from 0 to 1023, each once
- counts: int32 [8], P('grp'), parts along dimension 0, may hold values from 2 to 8, as said below
- delays: int32 [512, 1024], P(('grp', 'sub')), parts along dimension 0, may hold values from 0 to 127
- beam_owner: int32 [512, 1], P('grp'), parts along dimension 0, may hold values from 0 to 3; in each aligned block of 64 rows (0 to 63, 64 to 127, ...) at most 32 rows name the same one
Outputs:
- visibility: bfloat16 [256, 2, 1024, 1024], P(('grp', 'chan'), None, 'sub'), parts along dimension 0
- resynth: float32 [1024, 2, 5504], P(('grp', 'chan', 'sub')), parts along dimension 0
There are 2 independent parts, one for each index of `grp`. A program takes and returns all parts, laid end to end along the dimension named above; an argument that names none is the same for every part. Nothing has to cross between parts.
Inputs may be any that keep to these rules, and one draw needn't show every extreme that they name: `input_id`: each input id appears once. `counts`: every draw has a block with all 8 spectra valid. `beam_owner`: within each section of 64 consecutive beams no owner is named more than 32 times; some owner is named exactly 32 times in some section.
All inputs are finite; a program needn't handle non-finite values.
Results may differ from a plain program's by a relative error of at most 0.007.
Values may be sent and summed in bfloat16 or wider, within the bound.
A program may use at most 192 MiB of HBM per device.

v0:
```python
import math
import jax
import jax.numpy as jnp
from jax import lax
from jax.sharding import PartitionSpec as P

NCH = 128
TAPS = 12
SPEC = 8
BLOCKS = 4
BEAMS = 256


def filter_table(taps, chans):
    length = taps.shape[0]
    position = jnp.arange(length, dtype=jnp.int32) % chans
    channel = jnp.arange(chans, dtype=jnp.int32)
    phase = (position[:, None] * channel[None, :] % chans).astype(jnp.float32) * (
        2.0 * math.pi / chans
    )
    cosine = taps[:, None] * jnp.cos(phase)
    sine = taps[:, None] * jnp.sin(phase)
    upper = jnp.concatenate([cosine, -sine], axis=1)
    lower = jnp.concatenate([sine, cosine], axis=1)
    return jnp.concatenate([upper, lower], axis=0).astype(jnp.bfloat16)


def resynthesize(received, table, taps_count, chans):
    count = received.shape[0]
    spectra_n = received.shape[3]
    table3 = table.reshape(2 * taps_count * chans, 2, chans)
    grid = jnp.einsum("pcht,mch->ptm", received, table3, preferred_element_type=jnp.float32)
    grid = grid.reshape(count, spectra_n, 2, taps_count, chans)
    total = jnp.zeros((count, spectra_n + taps_count - 1, 2, chans), jnp.float32)
    for k in range(taps_count):
        total = total + jnp.pad(
            grid[:, :, :, k, :], ((0, 0), (k, taps_count - 1 - k), (0, 0), (0, 0))
        )
    return jnp.transpose(total, (0, 2, 1, 3)).reshape(
        count, 2, (spectra_n + taps_count - 1) * chans
    )


def local(voltages, taps, input_id, counts, delays, beam_owner):
    n_chan = lax.axis_size("chan")
    n_sub = lax.axis_size("sub")
    inp_dev = voltages.shape[0]
    inputs = input_id.shape[0]
    chans = NCH
    taps_count = TAPS
    spectra_n = BLOCKS * SPEC
    ch_dev = chans // n_chan
    rows = inputs // n_sub
    section = BEAMS // n_sub
    most = min(section, max(2, 2 * section // n_chan))
    table = filter_table(taps, chans)
    position = jnp.arange(spectra_n, dtype=jnp.int32)
    valid = (position % SPEC < jnp.repeat(counts, SPEC)).astype(jnp.float32)
    total = jnp.sum(counts.astype(jnp.float32))
    frames = voltages.reshape(inp_dev, 2, spectra_n + taps_count - 1, chans)
    windows = jnp.concatenate(
        [frames[:, :, k : k + spectra_n, :] for k in range(taps_count)], axis=3
    )
    table3 = table.reshape(2, taps_count * chans, 2 * chans)
    filtered = jnp.einsum("icth,chm->mit", windows, table3, preferred_element_type=jnp.float32)
    filtered = filtered * valid[None, None, :]
    spectra = filtered.reshape(2, chans, inp_dev, spectra_n).astype(jnp.bfloat16)
    slot_of = jnp.zeros((inputs,), jnp.int32).at[input_id].set(jnp.arange(inputs, dtype=jnp.int32))
    turned = lax.all_to_all(spectra, "chan", split_axis=1, concat_axis=2, tiled=True)
    gathered = lax.all_gather(turned, "sub", axis=2, tiled=True)
    chan_part = slot_of // (n_sub * inp_dev)
    sub_part = slot_of // inp_dev % n_sub
    order = (sub_part * n_chan + chan_part) * inp_dev + slot_of % inp_dev
    by_id = jnp.take(gathered, order, axis=2)
    sub_index = lax.axis_index("sub")
    mine = lax.dynamic_slice_in_dim(by_id, sub_index * rows, rows, 2)
    real_part = jnp.einsum("cxit,cxjt->xij", mine, by_id, preferred_element_type=jnp.float32)
    imag_part = jnp.einsum("xit,xjt->xij", mine[1], by_id[0], preferred_element_type=jnp.float32)
    imag_part = imag_part - jnp.einsum(
        "xit,xjt->xij", mine[0], by_id[1], preferred_element_type=jnp.float32
    )
    visibility = (jnp.stack([real_part, imag_part], axis=1) / total).astype(jnp.bfloat16)
    channel = lax.axis_index("chan") * ch_dev + jnp.arange(ch_dev, dtype=jnp.int32)
    phase = (delays[None, :, :] * channel[:, None, None] % chans).astype(jnp.float32) * (
        2.0 * math.pi / chans
    )
    scale = 1.0 / math.sqrt(inputs)
    weight_cos = (jnp.cos(phase) * scale).astype(jnp.bfloat16)
    weight_sin = (jnp.sin(phase) * scale).astype(jnp.bfloat16)
    from_cos = jnp.einsum("xbi,cxit->cxbt", weight_cos, by_id, preferred_element_type=jnp.float32)
    from_sin = jnp.einsum("xbi,cxit->cxbt", weight_sin, by_id, preferred_element_type=jnp.float32)
    beams = jnp.stack([from_cos[0] - from_sin[1], from_cos[1] + from_sin[0]]).astype(jnp.bfloat16)
    owner = lax.dynamic_slice_in_dim(beam_owner[:, 0], sub_index * section, section)
    beam = jnp.arange(section, dtype=jnp.int32)
    earlier = (owner[None, :] == owner[:, None]) & (beam[None, :] < beam[:, None])
    rank = jnp.sum(earlier.astype(jnp.int32), axis=1)
    target = owner * most + rank
    select = (jnp.arange(n_chan * most, dtype=jnp.int32)[:, None] == target[None, :]).astype(
        jnp.bfloat16
    )
    placed = jnp.einsum("pb,cxbt->pcxt", select, beams, preferred_element_type=jnp.float32).astype(
        jnp.bfloat16
    )
    placed = placed.reshape(n_chan, most, 2, ch_dev, spectra_n)
    resynth = resynthesize(
        lax.all_to_all(placed, "chan", split_axis=0, concat_axis=3, tiled=True)[0],
        table,
        taps_count,
        chans,
    )
    return (visibility, resynth)


def solution(mesh):
    placed = (
        P(("grp", "chan", "sub"), None, None),
        P(),
        P(),
        P("grp"),
        P(("grp", "sub"), None),
        P("grp", None),
    )
    return jax.shard_map(
        local,
        mesh=mesh,
        in_specs=placed,
        out_specs=(P(("grp", "chan"), None, "sub", None), P(("grp", "chan", "sub"), None, None)),
        check_vma=False,
    )
```

profile of v0, /device:TPU:0, one launch (start us, length us, event | category | flops | bytes accessed | tf_op | source)
XLA Modules:
  0.0 464.1 jit_solution(4813590015660750824)
XLA Ops:
  7.2 0.0 all-gather.2.cloned.1.call-start
  7.2 0.7 broadcast_in_dim.18
  7.9 0.1 reshape.202
  8.0 3.7 reshape.232
  11.7 0.0 copy-start.4
  11.7 3.5 fusion.74
  15.3 0.7 copy_dynamic-update-slice_fusion.11
  16.0 4.7 %negate_convert_fusion.1 = (bf16[1536,128]{1,0:T(8,128)(2,1)S(1)}, bf16[1536,128]{1,0:T(8,128)(2,1)S(1)}, bf16[1536,128]{1,0:T(8,128)(2,1)S(1)}) fusion(s32[1536]{0:T(1024)S(1)} %add_select_fusion.3, f32[1536]{0:T(1024)S(1)} %copy-done.4), kind=kLoop, calls=%fused_computation.79 | loop fusion | flops 3932160 | bytes 1191936 | tf_op jit(solution)/shard_map/convert.13
  20.7 0.9 copy_dynamic-update-slice_fusion.10
  21.5 0.9 copy_dynamic-update-slice_fusion.9
  22.4 0.9 copy_dynamic-update-slice_fusion.8
  23.2 0.9 copy_dynamic-update-slice_fusion.7
  24.1 0.9 copy_dynamic-update-slice_fusion.6
  25.0 0.9 copy_dynamic-update-slice_fusion.5
  25.8 0.9 copy_dynamic-update-slice_fusion.4
  26.7 0.9 copy_dynamic-update-slice_fusion.3
  27.6 0.9 copy_dynamic-update-slice_fusion.2
  28.4 0.9 copy_dynamic-update-slice_fusion.1
  29.3 0.9 copy_dynamic-update-slice_fusion
  30.2 4.8 %copy-done.3 = bf16[64,2,32,1536]{3,0,1,2:T(8,128)(2,1)} copy-done((bf16[64,2,32,1536]{3,0,1,2:T(8,128)(2,1)}, bf16[64,2,32,1536]{3,0,1,2:T(8,128)(2,1)S(1)}, u32[]{:S(2)}) %copy-start.3) | copy-done | bytes 12582936
  34.9 0.2 maximum_maximum_fusion
  35.1 8.2 %fusion.15 = bf16[256,64,32]{0,1,2:T(8,128)(2,1)S(1)} fusion(bf16[2,1536,256,1]{2,1,0,3:T(8,128)(2,1)S(1)} %bitcast.153, bf16[64,2,32,1536]{3,0,1,2:T(8,128)(2,1)} %copy-done.3, f32[32]{0:T(128)S(1)} %compare_convert_fusion), kind=kOutput, calls=%fused_computation.28 | convolution fusion | flops 3222274048 | bytes 15204480 | tf_op jit(solution)/shard_map/icth,chm->mit/dot_general | solution.py:65
  43.4 0.3 convert_element_type.100
  43.7 2.2 copy.105
  45.8 1.7 reshape.237
  47.5 32.0 %all_to_all.33 = bf16[4,2,65536]{2,1,0:T(2,128)(2,1)} all-to-all(bf16[4,2,65536]{2,1,0:T(2,128)(2,1)S(1)} %reshape.237), channel_id=1, replica_groups=mesh['grp'=2,'chan'=4,'sub'=4] {'chan'}, dimensions={0} | all-to-all | bytes 2097152 | tf_op jit(solution)/shard_map/all_to_all | solution.py:69
  79.5 3.1 reshape.238
  82.6 6.5 %copy.149 = bf16[2,32,4,64,32]{4,1,3,2,0:T(8,128)(2,1)} copy(bf16[2,32,4,64,32]{3,4,0,1,2:T(8,128)(2,1)S(1)} %bitcast.149) | data formatting | bytes 2097152 | tf_op jit(solution)/shard_map/all_to_all | solution.py:69
  89.1 0.0 all-gather.2.cloned.1.call-update
  89.2 4.3 scatter_custom_fusion
  93.5 0.1 dynamic-slice_bitcast_fusion.1
  93.6 0.6 convert_reduce_fusion.1
  94.2 0.2 convert_reduce_fusion
  94.4 0.1 multiply_add_fusion
  94.5 4.2 negate_convert_fusion
  98.7 1.3 maximum_maximum_fusion.1
  99.9 94.3 %all-gather.2.cloned.1.call-done = bf16[2,32,1024,32]{3,1,2,0:T(8,128)(2,1)} async-done(((bf16[2,32,256,32]{3,1,2,0:T(8,128)(2,1)}), bf16[2,32,1024,32]{3,1,2,0:T(8,128)(2,1)}) %all-gather.2.cloned.1.call-update) | async-done | bytes 4194320 | tf_op jit(solution)/shard_map/all_gather | solution.py:70
  194.3 19.1 %gather_fusion = bf16[1024,2,32,32]{3,2,1,0:T(8,128)(2,1)} fusion(bf16[2,32,1024,32]{3,1,2,0:T(8,128)(2,1)} %all-gather.2.cloned.1.call-done, s32[1024]{0:T(1024)S(1)} %broadcast_clamp_fusion), kind=kCustom, calls=%fused_computation | custom fusion | bytes 8392704 | tf_op jit(solution)/shard_map/jit(_take)/gather | solution.py:74
  213.4 17.5 %copy.109 = bf16[1024,2,32,32]{0,3,1,2:T(8,128)(2,1)} copy(bf16[1024,2,32,32]{3,2,1,0:T(8,128)(2,1)} %gather_fusion) | data formatting | bytes 8388608 | tf_op jit(solution)/shard_map/jit(_take)/gather | solution.py:74
  230.9 2.7 broadcast_select_fusion
  233.7 0.7 copy-done
  234.4 2.7 fusion.78
  237.0 31.8 %fusion.21 = f32[2,32,64,32]{2,3,0,1:T(8,128)S(1)} fusion(s32[32]{0:T(128)S(1)} %iota_add_fusion, s32[64,1024]{1,0:T(8,128)S(1)} %copy-done.8, bf16[1024,2,32,32]{0,3,1,2:T(8,128)(2,1)S(1)} %broadcast_select_fusion), kind=kOutput, calls=%fused_computation.35 | convolution fusion | flops 301989888 | bytes 4980864 | tf_op jit(solution)/shard_map/xbi,cxit->cxbt/dot_general | solution.py:90
  268.8 32.1 %fusion.18 = f32[2,32,64,32]{2,3,0,1:T(8,128)S(1)} fusion(s32[32]{0:T(128)S(1)} %iota_add_fusion, s32[64,1024]{1,0:T(8,128)S(1)} %copy-done.8, bf16[1024,2,32,32]{0,3,1,2:T(8,128)(2,1)S(1)} %broadcast_select_fusion), kind=kOutput, calls=%fused_computation.34 | convolution fusion | flops 301989888 | bytes 4980864 | tf_op jit(solution)/shard_map/xbi,cxit->cxbt/dot_general | solution.py:91
  300.9 0.2 dynamic-slice_bitcast_fusion
  301.1 0.2 fusion.39
  301.3 1.2 convolution_convert_fusion
  302.5 3.1 reshape.203
  305.6 1.7 copy.194
  307.3 4.5 reshape.239
  311.8 4.6 all-to-all-start.1
  316.4 15.5 %convolution_bitcast_fusion = f32[32,1,256,1024]{3,2,0,1:T(8,128)} fusion(bf16[2,32,256,32]{2,3,0,1:T(8,128)(2,1)S(1)} %dynamic-slice_bitcast_fusion, bf16[1024,2,32,32]{0,3,1,2:T(8,128)(2,1)} %copy-done.1), kind=kOutput, calls=%fused_computation.8 | convolution fusion | flops 1073741824 | bytes 38797312 | tf_op jit(solution)/shard_map/cxit,cxjt->xij/dot_general | solution.py:77
  331.8 14.0 %fusion.14 = f32[32,256,1024]{2,1,0:T(8,128)} fusion(bf16[2,32,1024,32]{2,3,0,1:T(8,128)(2,1)S(1)} %copy-done.2, bf16[2,32,256,32]{2,3,0,1:T(8,128)(2,1)S(1)} %dynamic-slice_bitcast_fusion), kind=kOutput, calls=%fused_computation.26 | convolution fusion | flops 536870912 | bytes 36175872 | tf_op jit(solution)/shard_map/xit,xjt->xij/dot_general | solution.py:78
  345.9 21.7 %subtract_bitcast_fusion = f32[32,1,256,1024]{3,2,0,1:T(8,128)} fusion(f32[32,256,1024]{2,1,0:T(8,128)} %fusion.14, bf16[2,32,1024,32]{2,3,0,1:T(8,128)(2,1)S(1)} %copy-done.2, bf16[2,32,256,32]{2,3,0,1:T(8,128)(2,1)S(1)} %dynamic-slice_bitcast_fusion), kind=kOutput, calls=%fused_computation.4 | convolution fusion | flops 545259520 | bytes 69730304 | tf_op jit(solution)/shard_map/xit,xjt->xij/dot_general | solution.py:79
  367.5 33.5 %fusion = bf16[32,2,256,1024]{3,2,0,1:T(8,128)(2,1)} fusion(f32[32,1,256,1024]{3,2,0,1:T(8,128)} %subtract_bitcast_fusion, f32[32,1,256,1024]{3,2,0,1:T(8,128)} %convolution_bitcast_fusion, f32[]{:T(128)} %convert_reduce_fusion.1), kind=kLoop, calls=%fused_computation.3 | loop fusion | flops 50331648 | bytes 100663296 | tf_op jit(solution)/shard_map/convert_element_type | solution.py:82
  401.1 23.2 %copy.126 = bf16[32,2,256,1024]{3,2,1,0:T(8,128)(2,1)} copy(bf16[32,2,256,1024]{3,2,0,1:T(8,128)(2,1)} %fusion) | data formatting | bytes 67108864
  424.3 1.1 reshape.240
  425.4 1.8 bitcast_bitcast_fusion
  427.2 5.2 %copy.112 = bf16[1,32,2,4,32,32]{4,3,5,2,1,0:T(4,128)(2,1)S(1)} copy(bf16[1,32,2,4,32,32]{1,5,4,2,3,0:T(8,128)(2,1)} %bitcast_bitcast_fusion) | data formatting | bytes 1048576 | tf_op jit(solution)/shard_map/all_to_all | solution.py:106
  432.5 1.1 reshape.229
  433.5 7.4 %convolution_bitcast_fusion.1 = f32[32,32,2,12,128]{4,1,3,2,0:T(8,128)} fusion(bf16[2,12,128,2,128]{4,2,1,0,3:T(8,128)(2,1)} %bitcast.152, bf16[32,2,128,32,1,1]{2,3,1,0,4,5:T(8,128)(2,1)S(1)} %reshape.229), kind=kOutput, calls=%fused_computation.16 | convolution fusion | flops 1610612736 | bytes 14680064 | tf_op jit(solution)/shard_map/pcht,mch->ptm/dot_general | solution.py:32
  440.9 9.1 %slice_bitcast_fusion.15 = (f32[32,32,2,128]{3,1,2,0:T(8,128)S(1)}, f32[32,32,2,128]{3,1,2,0:T(8,128)S(1)}, f32[32,32,2,128]{3,1,2,0:T(8,128)S(1)}, f32[32,32,2,...) fusion(f32[32,32,2,12,128]{4,1,3,2,0:T(8,128)} %convolution_bit, ...), kind=kLoop, calls=%fused_computation.54 | loop fusion | bytes 25165824 | tf_op jit(solution)/shard_map/squeeze | solution.py:37
  450.0 5.0 %add_bitcast_fusion = f32[32,2,43,128]{3,2,1,0:T(8,128)S(1)} fusion(f32[32,32,2,128]{3,1,2,0:T(8,128)} %get-tuple-element.22, f32[32,32,2,128]{3,1,2,0:T(8,128)} %get-tuple-element.23, f32[32,32,2,128]{3,1,2,0:T(8,128)S(1)} %get-tuple-element.13, f32[32,32,2,128]{3,1,2,0:T(8,128)S(1)} %get-tuple-element.14, f32[32,32,2,128]{3,1,2,0:T(8,128)S(1)} %get-tuple-element.15, ...), kind=kLoop, calls=%fused_computation.33 | loop fusion | flops 3874816 | bytes 13991936 | tf_op jit(solution)/shard_map/transpose | solution.py:39
  455.0 1.8 reshape.234
  (23 shorter events, 0.1 us)
Async XLA Ops:
  7.2 187.1 %all-gather.2.cloned.1.call-start = ((), (), s32[]{:S(2)}) async-start(), calls=%async_computation.2 | async-start | bytes 20971520 | tf_op jit(solution)/shard_map/all_gather | solution.py:70
  11.7 4.2 copy-start.4
  30.2 4.8 %copy-start.3 = (bf16[64,2,32,1536]{3,0,1,2:T(8,128)(2,1)}, bf16[64,2,32,1536]{3,0,1,2:T(8,128)(2,1)S(1)}, u32[]{:S(2)}) copy-start(bf16[64,2,32,1536]{3,0,1,2:T(8,128)(2,1)S(1)} %copy_dynamic-update-slice_fusion) | copy-start | bytes 37748740
  82.6 6.6 %copy-start.5 = (s32[1024]{0:T(1024)S(1)}, s32[1024]{0:T(1024)}, u32[]{:S(2)}) copy-start(s32[1024]{0:T(1024)} %param.8) | copy-start | bytes 12292
  82.6 10.9 %copy-start.7 = (s32[256,1]{0,1:T(1,128)S(1)}, s32[256,1]{0,1:T(1,128)}, u32[]{:S(2)}) copy-start(s32[256,1]{0,1:T(1,128)} %param.11) | copy-start | bytes 3076
  82.6 11.0 %copy-start.6 = (s32[4]{0:T(128)S(1)}, s32[4]{0:T(128)}, u32[]{:S(2)}) copy-start(s32[4]{0:T(128)} %param.9) | copy-start | bytes 52
  230.9 3.4 copy-start
  234.4 66.6 %copy-start.1 = (bf16[1024,2,32,32]{0,3,1,2:T(8,128)(2,1)}, bf16[1024,2,32,32]{0,3,1,2:T(8,128)(2,1)S(1)}, u32[]{:S(2)}) copy-start(bf16[1024,2,32,32]{0,3,1,2:T(8,128)(2,1)S(1)} %broadcast_select_fusion) | copy-start | bytes 12582916
  234.4 2.7 copy-start.8
  311.8 112.5 %all-to-all-start.1 = ((bf16[4,2,32768]{2,1,0:T(2,128)(2,1)}), bf16[4,2,32768]{2,1,0:T(2,128)(2,1)S(1)}, u32[]{:S(2)}, u32[]{:S(2)}) async-start(bf16[4,2,32768]{2,1,0:T(2,128)(2,1)} %reshape.239), calls=%async_computation.1 | async-start | bytes 1048576 | tf_op jit(solution)/shard_map/all_to_all | solution.py:106
  316.4 15.5 %copy-start.2 = (bf16[2,32,1024,32]{2,3,0,1:T(8,128)(2,1)S(1)}, bf16[2,32,1024,32]{2,3,0,1:T(8,128)(2,1)}, u32[]{:S(2)}) copy-start(bf16[2,32,1024,32]{2,3,0,1:T(8,128)(2,1)} %fusion.78) | copy-start | bytes 12582916
Sparse Core Ops, SparseCore 0:
  89.2 104.9 all-gather.1
where the time goes:
time: 469 us; the launch traced here: 464 us
  matrix products  132 us (28%)
  local copies, waits for them, and re-layouts  131 us (28%)
  waiting for transfers between devices  94.4 us (20%)
  other arithmetic  55.3 us (12%)
  blocking collectives  32 us (7%)
  between operations  14.9 us (3%)
    all_gather x1, waiting for transfers between devices, local(): gathered = lax.all_gather(turned, 'sub', axis=2, tiled=True)  94.3 us
    unnamed x34, local copies, waits for them, and re-layouts  48.3 us
    gather x2, local copies, waits for them, and re-layouts, local(): by_id = jnp.take(gathered, order, axis=2)  36.6 us
    convert_element_type x1, other arithmetic, local(): (jnp.stack([real_part, imag_part], axis=1) / total).astype(jnp.bfloat16)  33.5 us
    dot_general x1, matrix products, local(): jnp.einsum('xbi,cxit->cxbt', weight_sin, by_id, preferred_element_type=jn...  32.1 us
    all_to_all x1, blocking collectives, local(): lax.all_to_all(spectra, 'chan', split_axis=1, concat_axis=2, tiled=True)  32 us
    dot_general x1, matrix products, local(): jnp.einsum('xbi,cxit->cxbt', weight_cos, by_id, preferred_element_type=jn...  31.8 us
    dot_general x1, matrix products, local(): jnp.einsum('xit,xjt->xij', mine[0], by_id[1], preferred_element_type=jnp....  21.7 us
  transfers between devices with their start and end apart: 2, of which 1 were waited for; matrix products, arithmetic and copies ran while one was open for 26% of the time, Pallas kernels for 0%

commit v1 on v0

--- a/solution.py
+++ b/solution.py
@@ -67,7 +67,9 @@
     spectra = filtered.reshape(2, chans, inp_dev, spectra_n).astype(jnp.bfloat16)
     slot_of = jnp.zeros((inputs,), jnp.int32).at[input_id].set(jnp.arange(inputs, dtype=jnp.int32))
     turned = lax.all_to_all(spectra, "chan", split_axis=1, concat_axis=2, tiled=True)
-    gathered = lax.all_gather(turned, "sub", axis=2, tiled=True)
+    gathered = jnp.concatenate(
+        lax.all_to_all(jnp.stack([turned] * lax.axis_size("sub")), "sub", 0, 0), axis=2
+    )
     chan_part = slot_of // (n_sub * inp_dev)
     sub_part = slot_of // inp_dev % n_sub
     order = (sub_part * n_chan + chan_part) * inp_dev + slot_of % inp_dev

time: 469 us -> 429 us (0.915)
  waiting for transfers between devices: 94.4 us -> 37.4 us
  local copies, waits for them, and re-layouts: 131 us -> 158 us
  between operations: 14.9 us -> 1.47 us
    all_gather x1 -> x0, waiting for transfers between devices: 94.3 us -> none  [local(): gathered = lax.all_gather(turned, 'sub', axis=2, tiled=True)]
    all_to_all x0 -> x1, waiting for transfers between devices: none -> 37.4 us  [local(): lax.all_to_all(jnp.stack([turned] * lax.axis_size('sub')), 'sub', 0, 0)]
    reshape x0 -> x1, local copies, waits for them, and re-layouts: none -> 23.1 us  [local(): jnp.concatenate(lax.all_to_all(jnp.stack([turned] * lax.axis_size('sub'))...]
    another operation x0 -> x2, local copies, waits for them, and re-layouts: none -> 6.04 us  [local(): jnp.stack([turned] * lax.axis_size('sub'))]
    all_to_all x0 -> x1, starting transfers between devices: none -> 4.97 us  [local(): lax.all_to_all(jnp.stack([turned] * lax.axis_size('sub')), 'sub', 0, 0)]
  transfers between devices with their start and end apart: 2 -> 2, of which waited for: 1 -> 1; matrix products, arithmetic and copies ran while one was open for 26% -> 28% of each run, Pallas kernels for 0% -> 0%
where the time goes in v1:
time: 429 us; the launch traced here: 424 us
  local copies, waits for them, and re-layouts  158 us (37%)
  matrix products  132 us (31%)
  other arithmetic  55.4 us (13%)
  waiting for transfers between devices  37.4 us (9%)
  blocking collectives  32 us (7%)
  starting transfers between devices  8.44 us (2%)
    unnamed x34, local copies, waits for them, and re-layouts  48.3 us
    all_to_all x1, waiting for transfers between devices, local(): lax.all_to_all(jnp.stack([turned] * lax.axis_size('sub')), 'sub', 0, 0)  37.4 us
    gather x2, local copies, waits for them, and re-layouts, local(): by_id = jnp.take(gathered, order, axis=2)  36.7 us
    convert_element_type x1, other arithmetic, local(): (jnp.stack([real_part, imag_part], axis=1) / total).astype(jnp.bfloat16)  33.5 us
    dot_general x1, matrix products, local(): jnp.einsum('xbi,cxit->cxbt', weight_sin, by_id, preferred_element_type=jn...  32.1 us
    all_to_all x1, blocking collectives, local(): lax.all_to_all(spectra, 'chan', split_axis=1, concat_axis=2, tiled=True)  32 us
    dot_general x1, matrix products, local(): jnp.einsum('xbi,cxit->cxbt', weight_cos, by_id, preferred_element_type=jn...  31.8 us
    reshape x1, local copies, waits for them, and re-layouts, local(): jnp.concatenate(lax.all_to_all(jnp.stack([turned] * lax.axis_size('sub'))...  23.1 us
  transfers between devices with their start and end apart: 2, of which 1 were waited for; matrix products, arithmetic and copies ran while one was open for 28% of the time, Pallas kernels for 0%

profile of v1, /device:TPU:0, one launch (start us, length us, event | category | flops | bytes accessed | tf_op | source)
XLA Modules:
  0.0 424.2 jit_solution(11493541644977457212)
XLA Ops:
  0.6 0.7 broadcast_in_dim.18
  1.4 0.1 reshape.211
  1.5 3.7 reshape.243
  5.1 3.5 fusion.74
  8.7 0.7 copy_dynamic-update-slice_fusion.11
  9.4 4.7 %negate_convert_fusion.1 = (bf16[1536,128]{1,0:T(8,128)(2,1)S(1)}, bf16[1536,128]{1,0:T(8,128)(2,1)S(1)}, bf16[1536,128]{1,0:T(8,128)(2,1)S(1)}) fusion(s32[1536]{0:T(1024)S(1)} %add_select_fusion.3, f32[1536]{0:T(1024)S(1)} %copy-done.4), kind=kLoop, calls=%fused_computation.79 | loop fusion | flops 3932160 | bytes 1191936 | tf_op jit(solution)/shard_map/convert.13
  14.1 0.9 copy_dynamic-update-slice_fusion.10
  14.9 0.9 copy_dynamic-update-slice_fusion.9
  15.8 0.9 copy_dynamic-update-slice_fusion.8
  16.7 0.9 copy_dynamic-update-slice_fusion.7
  17.5 0.9 copy_dynamic-update-slice_fusion.6
  18.4 0.9 copy_dynamic-update-slice_fusion.5
  19.3 0.9 copy_dynamic-update-slice_fusion.4
  20.1 0.9 copy_dynamic-update-slice_fusion.3
  21.0 0.9 copy_dynamic-update-slice_fusion.2
  21.8 0.9 copy_dynamic-update-slice_fusion.1
  22.7 0.9 copy_dynamic-update-slice_fusion
  23.6 4.8 %copy-done.3 = bf16[64,2,32,1536]{3,0,1,2:T(8,128)(2,1)} copy-done((bf16[64,2,32,1536]{3,0,1,2:T(8,128)(2,1)}, bf16[64,2,32,1536]{3,0,1,2:T(8,128)(2,1)S(1)}, u32[]{:S(2)}) %copy-start.3) | copy-done | bytes 12582936
  28.4 0.2 maximum_maximum_fusion
  28.5 8.3 %fusion.15 = bf16[256,64,32]{0,1,2:T(8,128)(2,1)S(1)} fusion(bf16[2,1536,256,1]{2,1,0,3:T(8,128)(2,1)S(1)} %bitcast.156, bf16[64,2,32,1536]{3,0,1,2:T(8,128)(2,1)} %copy-done.3, f32[32]{0:T(128)S(1)} %compare_convert_fusion), kind=kOutput, calls=%fused_computation.28 | convolution fusion | flops 3222274048 | bytes 15204480 | tf_op jit(solution)/shard_map/icth,chm->mit/dot_general | solution.py:65
  36.8 0.3 convert_element_type.100
  37.1 2.2 copy.106
  39.3 1.7 reshape.248
  40.9 32.0 %all_to_all.35 = bf16[4,2,65536]{2,1,0:T(2,128)(2,1)} all-to-all(bf16[4,2,65536]{2,1,0:T(2,128)(2,1)S(1)} %reshape.248), channel_id=1, replica_groups=mesh['grp'=2,'chan'=4,'sub'=4] {'chan'}, dimensions={0} | all-to-all | bytes 2097152 | tf_op jit(solution)/shard_map/all_to_all | solution.py:69
  72.9 3.1 reshape.249
  76.0 4.0 copy.108
  80.0 3.5 stack.24
  83.5 2.6 stack.25
  86.1 5.0 %all-to-all-start.1 = ((bf16[4,2,32,256,32]{3,4,2,1,0:T(8,128)(2,1)}), bf16[4,2,32,256,32]{3,4,2,1,0:T(8,128)(2,1)}, u32[]{:S(2)}, u32[]{:S(2)}) async-start(bf16[4,2,32,256,32]{3,4,2,1,0:T(8,128)(2,1)} %stack.25), calls=%async_computation.1 | async-start | bytes 8388608 | tf_op jit(solution)/shard_map/all_to_all | solution.py:71
  91.1 4.3 %scatter_custom_fusion = s32[1024]{0:T(1024)S(1)} fusion(s32[1024]{0:T(1024)S(1)} %compare_select_fusion.1, s32[1024]{0:T(1024)S(1)} %iota.42, s32[]{:T(128)} %constant.113.clone.1), kind=kCustom, calls=%fused_computation.134 | custom fusion | bytes 4100 | tf_op jit(solution)/shard_map/scatter | solution.py:68
  95.5 0.6 convert_reduce_fusion.1
  96.2 0.2 convert_reduce_fusion
  96.3 0.1 multiply_add_fusion
  96.4 4.2 negate_convert_fusion
  100.6 1.3 maximum_maximum_fusion.1
  101.9 37.4 %all-to-all-done.1 = bf16[4,2,32,256,32]{3,4,2,1,0:T(8,128)(2,1)} async-done(((bf16[4,2,32,256,32]{3,4,2,1,0:T(8,128)(2,1)}), bf16[4,2,32,256,32]{3,4,2,1,0:T(8,128)(2,1)}, u32[]{:S(2)}, u32[]{:S(2)}) %all-to-all-start.1) | async-done | bytes 4194336 | tf_op jit(solution)/shard_map/all_to_all | solution.py:71
  139.3 23.1 %copy.151 = bf16[2,32,4,256,32]{4,1,3,2,0:T(8,128)(2,1)} copy(bf16[2,32,4,256,32]{3,4,1,0,2:T(8,128)(2,1)} %bitcast.7) | data formatting | bytes 8388608 | tf_op jit(solution)/shard_map/reshape | solution.py:70
  162.3 19.2 %gather_fusion = bf16[1024,2,32,32]{3,2,1,0:T(8,128)(2,1)} fusion(bf16[2,32,1024,32]{3,1,2,0:T(8,128)(2,1)} %bitcast.151, s32[1024]{0:T(1024)S(1)} %broadcast_clamp_fusion), kind=kCustom, calls=%fused_computation | custom fusion | bytes 8392704 | tf_op jit(solution)/shard_map/jit(_take)/gather | solution.py:76
  181.5 17.5 %copy.111 = bf16[1024,2,32,32]{0,3,1,2:T(8,128)(2,1)} copy(bf16[1024,2,32,32]{3,2,1,0:T(8,128)(2,1)} %gather_fusion) | data formatting | bytes 8388608 | tf_op jit(solution)/shard_map/jit(_take)/gather | solution.py:76
  199.0 2.7 broadcast_select_fusion
  201.8 0.7 copy-done
  202.5 2.7 fusion.78
  205.1 31.8 %fusion.21 = f32[2,32,64,32]{2,3,0,1:T(8,128)S(1)} fusion(s32[32]{0:T(128)S(1)} %iota_add_fusion, s32[64,1024]{1,0:T(8,128)S(1)} %copy-done.8, bf16[1024,2,32,32]{0,3,1,2:T(8,128)(2,1)S(1)} %broadcast_select_fusion), kind=kOutput, calls=%fused_computation.35 | convolution fusion | flops 301989888 | bytes 4980864 | tf_op jit(solution)/shard_map/xbi,cxit->cxbt/dot_general | solution.py:92
  236.9 32.1 %fusion.18 = f32[2,32,64,32]{2,3,0,1:T(8,128)S(1)} fusion(s32[32]{0:T(128)S(1)} %iota_add_fusion, s32[64,1024]{1,0:T(8,128)S(1)} %copy-done.8, bf16[1024,2,32,32]{0,3,1,2:T(8,128)(2,1)S(1)} %broadcast_select_fusion), kind=kOutput, calls=%fused_computation.34 | convolution fusion | flops 301989888 | bytes 4980864 | tf_op jit(solution)/shard_map/xbi,cxit->cxbt/dot_general | solution.py:93
  269.0 0.2 dynamic-slice_bitcast_fusion
  269.2 0.2 fusion.39
  269.4 1.2 convolution_convert_fusion
  270.6 3.1 reshape.214
  273.7 1.7 copy.196
  275.4 4.5 %reshape.250 = bf16[4,2,32768]{2,1,0:T(2,128)(2,1)} reshape(bf16[4,2,32,32,32]{4,3,2,1,0:T(8,128)(2,1)} %bitcast.153) | data formatting | bytes 1048576
  279.9 3.5 all-to-all-start.2
  283.3 15.5 %convolution_bitcast_fusion = f32[32,1,256,1024]{3,2,0,1:T(8,128)} fusion(bf16[2,32,256,32]{2,3,0,1:T(8,128)(2,1)S(1)} %dynamic-slice_bitcast_fusion, bf16[1024,2,32,32]{0,3,1,2:T(8,128)(2,1)} %copy-done.1), kind=kOutput, calls=%fused_computation.8 | convolution fusion | flops 1073741824 | bytes 38797312 | tf_op jit(solution)/shard_map/cxit,cxjt->xij/dot_general | solution.py:79
  298.8 14.0 %fusion.14 = f32[32,256,1024]{2,1,0:T(8,128)} fusion(bf16[2,32,1024,32]{2,3,0,1:T(8,128)(2,1)S(1)} %copy-done.2, bf16[2,32,256,32]{2,3,0,1:T(8,128)(2,1)S(1)} %dynamic-slice_bitcast_fusion), kind=kOutput, calls=%fused_computation.26 | convolution fusion | flops 536870912 | bytes 36175872 | tf_op jit(solution)/shard_map/xit,xjt->xij/dot_general | solution.py:80
  312.9 21.7 %subtract_bitcast_fusion = f32[32,1,256,1024]{3,2,0,1:T(8,128)} fusion(f32[32,256,1024]{2,1,0:T(8,128)} %fusion.14, bf16[2,32,1024,32]{2,3,0,1:T(8,128)(2,1)S(1)} %copy-done.2, bf16[2,32,256,32]{2,3,0,1:T(8,128)(2,1)S(1)} %dynamic-slice_bitcast_fusion), kind=kOutput, calls=%fused_computation.4 | convolution fusion | flops 545259520 | bytes 69730304 | tf_op jit(solution)/shard_map/xit,xjt->xij/dot_general | solution.py:81
  334.5 33.5 %fusion = bf16[32,2,256,1024]{3,2,0,1:T(8,128)(2,1)} fusion(f32[32,1,256,1024]{3,2,0,1:T(8,128)} %subtract_bitcast_fusion, f32[32,1,256,1024]{3,2,0,1:T(8,128)} %convolution_bitcast_fusion, f32[]{:T(128)} %convert_reduce_fusion.1), kind=kLoop, calls=%fused_computation.3 | loop fusion | flops 50331648 | bytes 100663296 | tf_op jit(solution)/shard_map/convert_element_type | solution.py:84
  368.1 23.2 %copy.128 = bf16[32,2,256,1024]{3,2,1,0:T(8,128)(2,1)} copy(bf16[32,2,256,1024]{3,2,0,1:T(8,128)(2,1)} %fusion) | data formatting | bytes 67108864
  391.3 1.1 reshape.251
  392.4 1.8 bitcast_bitcast_fusion
  394.2 5.2 %copy.114 = bf16[1,32,2,4,32,32]{4,3,5,2,1,0:T(4,128)(2,1)S(1)} copy(bf16[1,32,2,4,32,32]{1,5,4,2,3,0:T(8,128)(2,1)} %bitcast_bitcast_fusion) | data formatting | bytes 1048576 | tf_op jit(solution)/shard_map/all_to_all | solution.py:108
  399.5 1.1 reshape.240
  400.5 7.4 %convolution_bitcast_fusion.1 = f32[32,32,2,12,128]{4,1,3,2,0:T(8,128)} fusion(bf16[2,12,128,2,128]{4,2,1,0,3:T(8,128)(2,1)} %bitcast.155, bf16[32,2,128,32,1,1]{2,3,1,0,4,5:T(8,128)(2,1)S(1)} %reshape.240), kind=kOutput, calls=%fused_computation.16 | convolution fusion | flops 1610612736 | bytes 14680064 | tf_op jit(solution)/shard_map/pcht,mch->ptm/dot_general | solution.py:32
  407.9 9.1 %slice_bitcast_fusion.15 = (f32[32,32,2,128]{3,1,2,0:T(8,128)S(1)}, f32[32,32,2,128]{3,1,2,0:T(8,128)S(1)}, f32[32,32,2,128]{3,1,2,0:T(8,128)S(1)}, f32[32,32,2,...) fusion(f32[32,32,2,12,128]{4,1,3,2,0:T(8,128)} %convolution_bit, ...), kind=kLoop, calls=%fused_computation.54 | loop fusion | bytes 25165824 | tf_op jit(solution)/shard_map/squeeze | solution.py:37
  417.0 5.0 %add_bitcast_fusion = f32[32,2,43,128]{3,2,1,0:T(8,128)S(1)} fusion(f32[32,32,2,128]{3,1,2,0:T(8,128)} %get-tuple-element.22, f32[32,32,2,128]{3,1,2,0:T(8,128)} %get-tuple-element.23, f32[32,32,2,128]{3,1,2,0:T(8,128)S(1)} %get-tuple-element.13, f32[32,32,2,128]{3,1,2,0:T(8,128)S(1)} %get-tuple-element.14, f32[32,32,2,128]{3,1,2,0:T(8,128)S(1)} %get-tuple-element.15, ...), kind=kLoop, calls=%fused_computation.33 | loop fusion | flops 3874816 | bytes 13991936 | tf_op jit(solution)/shard_map/transpose | solution.py:39
  422.0 1.8 reshape.245
  (25 shorter events, 0.2 us)
Async XLA Ops:
  5.1 4.2 copy-start.4
  23.6 4.8 %copy-start.3 = (bf16[64,2,32,1536]{3,0,1,2:T(8,128)(2,1)}, bf16[64,2,32,1536]{3,0,1,2:T(8,128)(2,1)S(1)}, u32[]{:S(2)}) copy-start(bf16[64,2,32,1536]{3,0,1,2:T(8,128)(2,1)S(1)} %copy_dynamic-update-slice_fusion) | copy-start | bytes 37748740
  86.1 5.0 %copy-start.5 = (s32[1024]{0:T(1024)S(1)}, s32[1024]{0:T(1024)}, u32[]{:S(2)}) copy-start(s32[1024]{0:T(1024)} %param.8) | copy-start | bytes 12292
  86.1 9.4 %copy-start.7 = (s32[256,1]{0,1:T(1,128)S(1)}, s32[256,1]{0,1:T(1,128)}, u32[]{:S(2)}) copy-start(s32[256,1]{0,1:T(1,128)} %param.11) | copy-start | bytes 3076
  86.1 9.4 %copy-start.6 = (s32[4]{0:T(128)S(1)}, s32[4]{0:T(128)}, u32[]{:S(2)}) copy-start(s32[4]{0:T(128)} %param.9) | copy-start | bytes 52
  86.1 53.2 %all-to-all-start.1 = ((bf16[4,2,32,256,32]{3,4,2,1,0:T(8,128)(2,1)}), bf16[4,2,32,256,32]{3,4,2,1,0:T(8,128)(2,1)}, u32[]{:S(2)}, u32[]{:S(2)}) async-start(bf16[4,2,32,256,32]{3,4,2,1,0:T(8,128)(2,1)} %stack.25), calls=%async_computation.1 | async-start | bytes 8388608 | tf_op jit(solution)/shard_map/all_to_all | solution.py:71
  199.0 3.4 copy-start
  202.5 66.6 %copy-start.1 = (bf16[1024,2,32,32]{0,3,1,2:T(8,128)(2,1)}, bf16[1024,2,32,32]{0,3,1,2:T(8,128)(2,1)S(1)}, u32[]{:S(2)}) copy-start(bf16[1024,2,32,32]{0,3,1,2:T(8,128)(2,1)S(1)} %broadcast_select_fusion) | copy-start | bytes 12582916
  202.5 2.7 copy-start.8
  279.9 111.5 %all-to-all-start.2 = ((bf16[4,2,32768]{2,1,0:T(2,128)(2,1)}), bf16[4,2,32768]{2,1,0:T(2,128)(2,1)S(1)}, u32[]{:S(2)}, u32[]{:S(2)}) async-start(bf16[4,2,32768]{2,1,0:T(2,128)(2,1)} %reshape.250), calls=%async_computation.2 | async-start | bytes 1048576 | tf_op jit(solution)/shard_map/all_to_all | solution.py:108
  283.3 15.5 %copy-start.2 = (bf16[2,32,1024,32]{2,3,0,1:T(8,128)(2,1)S(1)}, bf16[2,32,1024,32]{2,3,0,1:T(8,128)(2,1)}, u32[]{:S(2)}) copy-start(bf16[2,32,1024,32]{2,3,0,1:T(8,128)(2,1)} %fusion.78) | copy-start | bytes 12582916
